TPU v7x, 512 devices: a whole 4x8x8 slice. The times are simulated.
512 devices in a mesh: row: 128 (over z, y, core), ex: 4 (over x).
Axes of the slice: x: 4, y: 8, z: 8, core: 2. Of those that a mesh axis runs over, the one named last changes fastest.
Arguments:
- grads: bfloat16 [1, 4, 2048, 2048], P(None, 'ex', 'row'), may hold values from -6 to 6
- right_inv: bfloat16 [2048, 2048], P('row', 'ex'), may hold values from -0.125 to 0.125
- left_inv: bfloat16 [2048, 2048], P(('row', 'ex')), may hold values from -0.125 to 0.125
- row_signs: int32 [1, 4, 2048], replicated, may hold values from 0 to 1
- col_signs: int32 [1, 4, 2048], replicated, may hold values from 0 to 1
- listed: int32 [1, 128, 4, 32], P(None, 'row', 'ex'), may hold values from 0 to 32767, as said below
- owners: int32 [1, 128, 4, 32, 1], P(None, 'row'), may hold values from 0 to 127; in each aligned block of 128 rows (0 to 127, 128 to 255, ..., all dimensions but the last counted through in order) at most 2 rows name the same one
Outputs:
- sketch: float32 [1, 128, 128, 2, 256], P(None, 'row')
Inputs may be any that keep to these rules, and one draw needn't show every extreme that they name: `listed`: for each batch b, group g and example x, the 32 entries name distinct blocks in ascending order, all from g * 256 to (g + 1) * 256 - 1. `owners`: within one batch and group, no owner is named by more than 2 of the 128 entries, a bound that some block reaches.
All inputs are finite; a program needn't handle non-finite values.
Results may differ from a plain program's by a relative error of at most 0.0029.
Values may be sent and summed in bfloat16 or wider, within the bound.
No kernel may reach another device: no remote copies, remote signals or barrier semaphores. Data moves between devices by JAX's collectives and lax.ppermute only.
A program may use at most 64 MiB of HBM per device.

v0:
```python
import math
import jax
import jax.numpy as jnp
from jax import lax
from jax.sharding import PartitionSpec as P

FA = 32
FB = 64
BLOCK = 128
highest = lax.Precision.HIGHEST


def dft_tables(length):
    counter = jnp.arange(length, dtype=jnp.int32)
    phase_index = counter[:, None] * counter[None, :] % length
    angles = phase_index.astype(jnp.float32) * (2.0 * math.pi / length)
    return (jnp.cos(angles), -jnp.sin(angles))


def twiddle_table(first_len, second_len, total):
    phase_index = (
        jnp.arange(first_len, dtype=jnp.int32)[:, None]
        * jnp.arange(second_len, dtype=jnp.int32)[None, :]
    )
    angles = phase_index.astype(jnp.float32) * (2.0 * math.pi / total)
    return (jnp.cos(angles), -jnp.sin(angles))


def complex_mul(real_a, imag_a, real_b, imag_b):
    return (real_a * real_b - imag_a * imag_b, real_a * imag_b + imag_a * real_b)


def column_transform(flipped, tables):
    first_cos, first_sin, mid_cos, mid_sin, last_cos, last_sin = tables
    lanes = flipped.shape[0]
    spatial = flipped.reshape(lanes, FA, FB)
    real_one = jnp.einsum("pk,jpq->jkq", first_cos, spatial, precision=highest)
    imag_one = jnp.einsum("pk,jpq->jkq", first_sin, spatial, precision=highest)
    real_two, imag_two = complex_mul(real_one, imag_one, mid_cos[None], mid_sin[None])
    real_out = jnp.einsum("qm,jkq->jmk", last_cos, real_two, precision=highest) - jnp.einsum(
        "qm,jkq->jmk", last_sin, imag_two, precision=highest
    )
    imag_out = jnp.einsum("qm,jkq->jmk", last_sin, real_two, precision=highest) + jnp.einsum(
        "qm,jkq->jmk", last_cos, imag_two, precision=highest
    )
    return (real_out.reshape(lanes, FA * FB), imag_out.reshape(lanes, FA * FB))


def row_transform(real_in, imag_in, tables):
    first_cos, first_sin, mid_cos, mid_sin, last_cos, last_sin = tables
    lanes = real_in.shape[1]
    real_grid = real_in.reshape(FA, FB, lanes)
    imag_grid = imag_in.reshape(FA, FB, lanes)
    real_one = jnp.einsum("pk,pql->kql", first_cos, real_grid, precision=highest) - jnp.einsum(
        "pk,pql->kql", first_sin, imag_grid, precision=highest
    )
    imag_one = jnp.einsum("pk,pql->kql", first_sin, real_grid, precision=highest) + jnp.einsum(
        "pk,pql->kql", first_cos, imag_grid, precision=highest
    )
    real_two, imag_two = complex_mul(real_one, imag_one, mid_cos[:, :, None], mid_sin[:, :, None])
    real_out = jnp.einsum("qm,kql->lmk", last_cos, real_two, precision=highest) - jnp.einsum(
        "qm,kql->lmk", last_sin, imag_two, precision=highest
    )
    imag_out = jnp.einsum("qm,kql->lmk", last_sin, real_two, precision=highest) + jnp.einsum(
        "qm,kql->lmk", last_cos, imag_two, precision=highest
    )
    return (real_out.reshape(lanes, FA * FB), imag_out.reshape(lanes, FA * FB))


def shards(grads, right_inv, left_inv, row_signs, col_signs, listed, owners):
    row_count = lax.axis_size("row")
    ex_count = lax.axis_size("ex")
    row_id = lax.axis_index("row")
    ex_id = lax.axis_index("ex")
    local_rows = grads.shape[2]
    width = grads.shape[3]
    ex_cols = right_inv.shape[1]
    list_len = listed.shape[3]
    block_count = local_rows * (width // BLOCK)
    capacity = max(2, 2 * ex_count * list_len // row_count)
    right_cols = lax.all_gather(right_inv, "row", axis=0, tiled=True)
    left_full = lax.all_gather(left_inv, ("row", "ex"), axis=0, tiled=True)
    pair_start = row_id * local_rows
    my_example = pair_start // ex_cols
    col_start = ex_id * ex_cols + pair_start % ex_cols
    first_cos, first_sin = dft_tables(FA)
    mid_cos, mid_sin = twiddle_table(FA, FB, width)
    last_cos, last_sin = dft_tables(FB)
    tables = (first_cos, first_sin, mid_cos, mid_sin, last_cos, last_sin)
    columns = col_start + jnp.arange(local_rows, dtype=jnp.int32)
    cross_phase = columns[:, None] * jnp.arange(width, dtype=jnp.int32)[None, :]
    cross_angle = cross_phase.astype(jnp.float32) * (2.0 * math.pi / (width * width))
    cross_cos = jnp.cos(cross_angle)
    cross_sin = -jnp.sin(cross_angle)
    entry_order = jnp.arange(ex_count * list_len, dtype=jnp.int32)
    before = entry_order[:, None] < entry_order[None, :]
    own_rows = grads[0]
    rows_all = lax.all_gather(own_rows, "ex", axis=0, tiled=True)
    projected = jnp.einsum(
        "xrk,kc->xcr", rows_all, right_cols, preferred_element_type=jnp.float32
    ).astype(jnp.bfloat16)
    projected = projected.reshape(ex_count * ex_cols, local_rows)
    pair_cols = lax.all_to_all(projected, "row", split_axis=0, concat_axis=1, tiled=True)
    whitened = lax.dot_general(
        pair_cols, left_full, (((1,), (1,)), ((), ())), preferred_element_type=jnp.float32
    )
    row_bits = lax.dynamic_index_in_dim(row_signs[0], my_example, 0, keepdims=False)
    col_bits = lax.dynamic_slice(col_signs[0], (my_example, col_start), (1, local_rows))[0]
    row_flip = (1 - 2 * row_bits).astype(jnp.float32)
    col_flip = (1 - 2 * col_bits).astype(jnp.float32)
    flipped = whitened * row_flip[None, :] * col_flip[:, None]
    real_one, imag_one = column_transform(flipped, tables)
    real_two, imag_two = complex_mul(real_one, imag_one, cross_cos, cross_sin)
    stacked = jnp.stack([real_two, imag_two])
    arrived_rows = lax.all_to_all(
        lax.all_to_all(stacked, "row", split_axis=2, concat_axis=1, tiled=True),
        "ex",
        split_axis=1,
        concat_axis=1,
        tiled=True,
    )
    real_four, imag_four = row_transform(arrived_rows[0], arrived_rows[1], tables)
    real_four = real_four / width
    imag_four = imag_four / width
    packed = jnp.concatenate(
        [real_four.reshape(block_count, BLOCK), imag_four.reshape(block_count, BLOCK)], axis=1
    )
    local_ids = listed[0, 0, 0] - row_id * block_count
    picked = jnp.take(packed, local_ids, axis=0)
    entries = lax.all_gather(picked, "ex", axis=0, tiled=True)
    owner_ids = owners[0, 0, :, :, 0].reshape(-1)
    same = owner_ids[:, None] == owner_ids[None, :]
    slot_index = jnp.sum(same & before, axis=0)
    position = owner_ids * capacity + slot_index
    outgoing = jnp.zeros((row_count * capacity, 2 * BLOCK), jnp.float32).at[position].set(entries)
    arrived = lax.all_to_all(outgoing, "row", split_axis=0, concat_axis=0, tiled=True)
    stores = [arrived.reshape(1, row_count, capacity, 2 * BLOCK)]
    return jnp.stack(stores)


def solution(mesh):
    in_specs = (
        P(None, "ex", "row", None),
        P("row", "ex"),
        P(("row", "ex"), None),
        P(),
        P(),
        P(None, "row", "ex", None),
        P(None, "row", None, None, None),
    )
    out_specs = P(None, "row", None, None, None)
    return jax.shard_map(shards, mesh=mesh, in_specs=in_specs, out_specs=out_specs, check_vma=False)
```

profile of v0, /device:TPU:1, one launch (start us, length us, event | category | flops | bytes accessed | tf_op | source)
XLA Modules:
  0.0 361.3 jit_solution(6742715925657476330)
XLA Ops:
  6.5 0.7 all-gather.5.cloned.1.call-update
  7.3 0.7 all-gather.7.cloned.1.call-update
  8.0 10.7 %all-gather = bf16[4,1,16,2048]{3,2,1,0:T(8,128)(2,1)S(1)} all-gather(bf16[1,1,16,2048]{3,2,1,0:T(8,128)(2,1)} %param.7), channel_id=2, replica_groups=mesh['row'=128,'ex'=4] {'ex'}, dimensions={0}, use_global_device_ids=true | all-gather | bytes 327680 | tf_op jit(solution)/shard_map/all_gather | solution.py:98
  18.8 0.7 fusion.70
  19.5 0.8 subtract_convert_fusion
  20.2 79.2 %all-gather.5.cloned.1.call-done = bf16[2048,512]{1,0:T(8,128)(2,1)} async-done(((bf16[16,512]{1,0:T(8,128)(2,1)}), bf16[2048,512]{1,0:T(8,128)(2,1)}) %all-gather.5.cloned.1.call-update) | async-done | bytes 2097168 | tf_op jit(solution)/shard_map/all_gather | solution.py:81
  99.4 2.1 fusion.12
  102.3 1.0 reshape.326
  103.3 9.4 %all-to-all-start = ((bf16[128,2,128]{2,1,0:T(2,128)(2,1)}), bf16[128,2,128]{2,1,0:T(2,128)(2,1)S(1)}, u32[]{:S(2)}, u32[]{:S(2)}) async-start(bf16[128,2,128]{2,1,0:T(2,128)(2,1)} %reshape.326), calls=%async_computation | async-start | bytes 131072 | tf_op jit(solution)/shard_map/all_to_all | solution.py:103
  112.7 0.8 convert_bitcast_fusion
  113.6 10.6 %all-to-all-done = bf16[128,2,128]{2,1,0:T(2,128)(2,1)S(1)} async-done(((bf16[128,2,128]{2,1,0:T(2,128)(2,1)}), bf16[128,2,128]{2,1,0:T(2,128)(2,1)S(1)}, u32[]{:S(2)}, u32[]{:S(2)}) %all-to-all-start) | async-done | bytes 65568 | tf_op jit(solution)/shard_map/all_to_all | solution.py:103
  124.5 104.7 %all-gather.7.cloned.1.call-done = bf16[512,4,2048]{2,1,0:T(4,128)(2,1)} async-done(((bf16[1,4,2048]{2,1,0:T(4,128)(2,1)}), bf16[512,4,2048]{2,1,0:T(4,128)(2,1)}) %all-gather.7.cloned.1.call-update) | async-done | bytes 8388624 | tf_op jit(solution)/shard_map/all_gather | solution.py:82
  229.2 12.5 %reshape.304 = bf16[2048,2048]{1,0:T(8,128)(2,1)} reshape(bf16[512,4,2048]{2,1,0:T(4,128)(2,1)} %all-gather.7.cloned.1.call-done) | data formatting | bytes 16777216
  241.7 5.6 %fusion = f32[16,2048]{1,0:T(8,128)S(1)} fusion(bf16[16,2048]{0,1:T(8,128)(2,1)S(1)} %bitcast.111, bf16[2048,2048]{1,0:T(8,128)(2,1)} %reshape.304, f32[16]{0:T(128)S(1)} %convert_bitcast_fusion, f32[2048]{0:T(1024)S(1)} %bitcast.113), kind=kOutput, calls=%fused_computation.3 | convolution fusion | flops 134283264 | bytes 8593472 | tf_op jit(solution)/shard_map/dot_general | solution.py:104
  247.5 0.5 convolution_bitcast_fusion
  247.9 0.4 convolution_bitcast_fusion.1
  248.4 0.5 fusion.20
  248.9 0.5 fusion.19
  249.4 0.5 fusion.8
  250.4 0.5 fusion.7
  251.3 0.6 multiply_subtract_fusion.2
  252.0 1.0 copy.35
  253.0 3.6 reshape.328
  256.6 10.0 %all-to-all-start.1 = ((f32[128,1,512]{2,1,0:T(1,128)}), f32[128,1,512]{2,1,0:T(1,128)S(1)}, u32[]{:S(2)}, u32[]{:S(2)}) async-start(f32[128,1,512]{2,1,0:T(1,128)} %reshape.328), calls=%async_computation.1 | async-start | bytes 524288 | tf_op jit(solution)/shard_map/all_to_all | solution.py:116
  266.6 0.5 broadcast.267
  267.1 0.7 fusion.127
  268.1 13.7 %all-to-all-done.1 = f32[128,1,512]{2,1,0:T(1,128)S(1)} async-done(((f32[128,1,512]{2,1,0:T(1,128)}), f32[128,1,512]{2,1,0:T(1,128)S(1)}, u32[]{:S(2)}, u32[]{:S(2)}) %all-to-all-start.1) | async-done | bytes 262176 | tf_op jit(solution)/shard_map/all_to_all | solution.py:116
  281.8 0.5 broadcast.268
  282.3 1.2 reduce.9
  283.6 2.8 reshape.329
  286.4 2.6 copy.51
  288.9 3.2 copy.46
  292.2 3.6 reshape.330
  295.8 3.7 %all-to-all-start.2 = ((f32[4,1,16384]{2,1,0:T(1,128)}), f32[4,1,16384]{2,1,0:T(1,128)S(1)}, u32[]{:S(2)}, u32[]{:S(2)}) async-start(f32[4,1,16384]{2,1,0:T(1,128)} %reshape.330), calls=%async_computation.2 | async-start | bytes 524288 | tf_op jit(solution)/shard_map/all_to_all | solution.py:115
  299.5 5.8 %all-to-all-done.2 = f32[4,1,16384]{2,1,0:T(1,128)S(1)} async-done(((f32[4,1,16384]{2,1,0:T(1,128)}), f32[4,1,16384]{2,1,0:T(1,128)S(1)}, u32[]{:S(2)}, u32[]{:S(2)}) %all-to-all-start.2) | async-done | bytes 262176 | tf_op jit(solution)/shard_map/all_to_all | solution.py:115
  305.3 1.3 reduce.10
  306.6 2.8 reshape.331
  309.4 2.4 fusion.128
  311.9 1.6 copy.47
  315.6 0.5 fusion.22
  316.1 0.5 fusion.21
  316.6 0.5 fusion.6
  317.5 0.5 fusion.4
  318.4 0.6 gather_fusion
  319.1 9.5 %all_gather.15 = f32[128,256]{1,0:T(8,128)S(1)} all-gather(f32[32,256]{1,0:T(8,128)S(1)} %broadcast_select_fusion), channel_id=1, replica_groups=mesh['row'=128,'ex'=4] {'ex'}, dimensions={0}, use_global_device_ids=true | all-gather | bytes 163840 | tf_op jit(solution)/shard_map/all_gather | solution.py:130
  328.6 1.1 scatter_custom_fusion
  329.8 24.0 %all_to_all.51 = f32[128,2,256]{2,1,0:T(2,128)S(1)} all-to-all(f32[128,2,256]{2,1,0:T(2,128)S(1)} %all_to_all.45), channel_id=1, replica_groups=mesh['row'=128,'ex'=4] {'row'}, dimensions={0} | all-to-all | bytes 524288 | tf_op jit(solution)/shard_map/all_to_all | solution.py:136
  353.8 0.7 copy.54
  (36 shorter events, 5.7 us)
Async XLA Ops:
  6.5 92.9 %all-gather.5.cloned.1.call-start = ((), (), s32[]{:S(2)}) async-start(), calls=%async_computation.4 | async-start | bytes 2113536 | tf_op jit(solution)/shard_map/all_gather | solution.py:81
  7.3 222.0 %all-gather.7.cloned.1.call-start = ((), (), s32[]{:S(2)}) async-start(), calls=%async_computation.5 | async-start | bytes 8404992 | tf_op jit(solution)/shard_map/all_gather | solution.py:82
  103.3 20.9 %all-to-all-start = ((bf16[128,2,128]{2,1,0:T(2,128)(2,1)}), bf16[128,2,128]{2,1,0:T(2,128)(2,1)S(1)}, u32[]{:S(2)}, u32[]{:S(2)}) async-start(bf16[128,2,128]{2,1,0:T(2,128)(2,1)} %reshape.326), calls=%async_computation | async-start | bytes 131072 | tf_op jit(solution)/shard_map/all_to_all | solution.py:103
  251.9 15.2 %copy-start = (s32[1,1,4,32,1]{3,4,2,1,0:T(1,128)S(1)}, s32[1,1,4,32,1]{3,4,2,1,0:T(1,128)}, u32[]{:S(2)}) copy-start(s32[1,1,4,32,1]{3,4,2,1,0:T(1,128)} %param.13) | copy-start | bytes 1540
  256.6 25.2 %all-to-all-start.1 = ((f32[128,1,512]{2,1,0:T(1,128)}), f32[128,1,512]{2,1,0:T(1,128)S(1)}, u32[]{:S(2)}, u32[]{:S(2)}) async-start(f32[128,1,512]{2,1,0:T(1,128)} %reshape.328), calls=%async_computation.1 | async-start | bytes 524288 | tf_op jit(solution)/shard_map/all_to_all | solution.py:116
  292.2 7.3 %copy-start.1 = (s32[1,1,1,32]{3,2,1,0:T(1,128)S(1)}, s32[1,1,1,32]{3,2,1,0:T(1,128)}, u32[]{:S(2)}) copy-start(s32[1,1,1,32]{3,2,1,0:T(1,128)} %param.12) | copy-start | bytes 388
  295.8 9.5 %all-to-all-start.2 = ((f32[4,1,16384]{2,1,0:T(1,128)}), f32[4,1,16384]{2,1,0:T(1,128)S(1)}, u32[]{:S(2)}, u32[]{:S(2)}) async-start(f32[4,1,16384]{2,1,0:T(1,128)} %reshape.330), calls=%async_computation.2 | async-start | bytes 524288 | tf_op jit(solution)/shard_map/all_to_all | solution.py:115
Sparse Core Ops, SparseCore 0:
  10.5 88.9 all-gather.4
  103.9 125.2 all-gather.6
where the time goes:
time: 362 us; the launch traced here: 361 us
  waiting for transfers between devices  215 us (59%)
  blocking collectives  44.2 us (12%)
  local copies, waits for them, and re-layouts  44.1 us (12%)
  starting transfers between devices  23.1 us (6%)
  matrix products  14.3 us (4%)
  between operations  13.8 us (4%)
  other arithmetic  6.33 us (2%)
    all_gather x1, waiting for transfers between devices, shards(): left_full = lax.all_gather(left_inv, ('row', 'ex'), axis=0, tiled=True)  105 us
    all_gather x1, waiting for transfers between devices, shards(): right_cols = lax.all_gather(right_inv, 'row', axis=0, tiled=True)  79.2 us
    unnamed x13, local copies, waits for them, and re-layouts  27.9 us
    all_to_all x1, blocking collectives, shards(): lax.all_to_all(outgoing, 'row', split_axis=0, concat_axis=0, tiled=True)  24 us
    all_to_all x1, waiting for transfers between devices, shards(): lax.all_to_all(stacked, 'row', split_axis=2, concat_axis=1, tiled=True)  13.7 us
    all_gather x1, blocking collectives, shards(): rows_all = lax.all_gather(own_rows, 'ex', axis=0, tiled=True)  10.7 us
    all_to_all x1, waiting for transfers between devices, shards(): lax.all_to_all(projected, 'row', split_axis=0, concat_axis=1, tiled=True)  10.6 us
    all_to_all x1, starting transfers between devices, shards(): lax.all_to_all(stacked, 'row', split_axis=2, concat_axis=1, tiled=True)  9.99 us
  transfers between devices with their start and end apart: 5, of which 5 were waited for; matrix products, arithmetic and copies ran while one was open for 2% of the time, Pallas kernels for 0%

commit v1 on v0

--- a/solution.py
+++ b/solution.py
@@ -79,7 +79,10 @@
     block_count = local_rows * (width // BLOCK)
     capacity = max(2, 2 * ex_count * list_len // row_count)
     right_cols = lax.all_gather(right_inv, "row", axis=0, tiled=True)
-    left_full = lax.all_gather(left_inv, ("row", "ex"), axis=0, tiled=True)
+    left_full = jnp.concatenate(
+        lax.all_to_all(jnp.stack([left_inv] * lax.axis_size(("row", "ex"))), ("row", "ex"), 0, 0),
+        axis=0,
+    )
     pair_start = row_id * local_rows
     my_example = pair_start // ex_cols
     col_start = ex_id * ex_cols + pair_start % ex_cols

time: 362 us -> 469 us (1.30); the launches traced: 361 us -> 462 us
  waiting for transfers between devices: 215 us -> 286 us
  blocking collectives: 44.2 us -> 65 us
  local copies, waits for them, and re-layouts: 44.1 us -> 51.1 us
    all_to_all x1, waiting for transfers between devices: 10.6 us -> 184 us  [shards(): lax.all_to_all(jnp.stack([left_inv] * lax.axis_size(('row', 'ex'))), ('ro...]
    all_gather x1 -> x0, waiting for transfers between devices: 105 us -> none  [shards(): left_full = lax.all_gather(left_inv, ('row', 'ex'), axis=0, tiled=True)]
    all_to_all x0 -> x1, blocking collectives: none -> 20.8 us  [shards(): lax.all_to_all(projected, 'row', split_axis=0, concat_axis=1, tiled=True)]
    unnamed x13 -> x14, local copies, waits for them, and re-layouts: 27.9 us -> 14.8 us
    reshape x0 -> x1, local copies, waits for them, and re-layouts: none -> 12.5 us  [shards(): jnp.concatenate(lax.all_to_all(jnp.stack([left_inv] * lax.axis_size(('row...]
    another operation x0 -> x1, local copies, waits for them, and re-layouts: none -> 7.49 us  [shards(): jnp.stack([left_inv] * lax.axis_size(('row', 'ex')))]
  transfers between devices with their start and end apart: 5 -> 4, of which waited for: 5 -> 4; matrix products, arithmetic and copies ran while one was open for 2% -> 1% of each run, Pallas kernels for 0% -> 0%
where the time goes in v1:
time: 469 us; the launch traced here: 462 us
  waiting for transfers between devices  286 us (61%)
  blocking collectives  65 us (14%)
  local copies, waits for them, and re-layouts  51.1 us (11%)
  starting transfers between devices  26.5 us (6%)
  matrix products  14.3 us (3%)
  between operations  14 us (3%)
  other arithmetic  5.74 us (1%)
    all_to_all x1, waiting for transfers between devices, shards(): lax.all_to_all(jnp.stack([left_inv] * lax.axis_size(('row', 'ex'))), ('ro...  184 us
    all_gather x1, waiting for transfers between devices, shards(): right_cols = lax.all_gather(right_inv, 'row', axis=0, tiled=True)  81.5 us
    all_to_all x1, blocking collectives, shards(): lax.all_to_all(outgoing, 'row', split_axis=0, concat_axis=0, tiled=True)  24 us
    all_to_all x1, blocking collectives, shards(): lax.all_to_all(projected, 'row', split_axis=0, concat_axis=1, tiled=True)  20.8 us
    unnamed x14, local copies, waits for them, and re-layouts  14.8 us
    all_to_all x1, waiting for transfers between devices, shards(): lax.all_to_all(stacked, 'row', split_axis=2, concat_axis=1, tiled=True)  13.5 us
    reshape x1, local copies, waits for them, and re-layouts, shards(): jnp.concatenate(lax.all_to_all(jnp.stack([left_inv] * lax.axis_size(('row...  12.5 us
    all_to_all x1, starting transfers between devices, shards(): lax.all_to_all(jnp.stack([left_inv] * lax.axis_size(('row', 'ex'))), ('ro...  12.3 us
  transfers between devices with their start and end apart: 4, of which 4 were waited for; matrix products, arithmetic and copies ran while one was open for 1% of the time, Pallas kernels for 0%

profile of v1, /device:TPU:1, one launch (start us, length us, event | category | flops | bytes accessed | tf_op | source)
XLA Modules:
  0.0 462.2 jit_solution(3392728466933052697)
XLA Ops:
  6.5 0.7 all-gather.3.cloned.1.call-update
  7.3 10.7 %all-gather = bf16[4,1,16,2048]{3,2,1,0:T(8,128)(2,1)S(1)} all-gather(bf16[1,1,16,2048]{3,2,1,0:T(8,128)(2,1)} %param.7), channel_id=2, replica_groups=mesh['row'=128,'ex'=4] {'ex'}, dimensions={0}, use_global_device_ids=true | all-gather | bytes 327680 | tf_op jit(solution)/shard_map/all_gather | solution.py:101
  18.0 81.5 %all-gather.3.cloned.1.call-done = bf16[2048,512]{1,0:T(8,128)(2,1)} async-done(((bf16[16,512]{1,0:T(8,128)(2,1)}), bf16[2048,512]{1,0:T(8,128)(2,1)}) %all-gather.3.cloned.1.call-update) | async-done | bytes 2097168 | tf_op jit(solution)/shard_map/all_gather | solution.py:81
  99.5 2.1 fusion.12
  102.7 20.8 %all_to_all.56 = bf16[128,2,128]{2,1,0:T(2,128)(2,1)S(1)} all-to-all(bf16[128,2,128]{2,1,0:T(2,128)(2,1)S(1)} %reshape.330), channel_id=1, replica_groups=mesh['row'=128,'ex'=4] {'row'}, dimensions={0} | all-to-all | bytes 131072 | tf_op jit(solution)/shard_map/all_to_all | solution.py:106
  123.5 7.5 %stack.4 = bf16[512,4,2048]{2,1,0:T(4,128)(2,1)} broadcast(bf16[4,2048]{1,0:T(4,128)(2,1)S(1)} %copy-done), dimensions={1,2} | broadcast | bytes 8404992 | tf_op jit(solution)/shard_map/stack | solution.py:83
  131.0 12.3 %all-to-all-start.1 = ((bf16[512,4,2048]{2,1,0:T(4,128)(2,1)}), bf16[512,4,2048]{2,1,0:T(4,128)(2,1)}, u32[]{:S(2)}, u32[]{:S(2)}) async-start(bf16[512,4,2048]{2,1,0:T(4,128)(2,1)} %stack.4), calls=%async_computation.1 | async-start | bytes 16777216 | tf_op jit(solution)/shard_map/all_to_all | solution.py:83
  143.3 0.8 convert_bitcast_fusion
  144.2 0.8 subtract_convert_fusion
  145.3 183.8 %all-to-all-done.1 = bf16[512,4,2048]{2,1,0:T(4,128)(2,1)} async-done(((bf16[512,4,2048]{2,1,0:T(4,128)(2,1)}), bf16[512,4,2048]{2,1,0:T(4,128)(2,1)}, u32[]{:S(2)}, u32[]{:S(2)}) %all-to-all-start.1) | async-done | bytes 8388640 | tf_op jit(solution)/shard_map/all_to_all | solution.py:83
  329.1 12.5 %reshape.288 = bf16[2048,2048]{1,0:T(8,128)(2,1)} reshape(bf16[512,4,2048]{2,1,0:T(4,128)(2,1)} %all-to-all-done.1) | data formatting | bytes 16777216 | tf_op jit(solution)/shard_map/reshape | solution.py:82
  341.6 5.6 %fusion = f32[16,2048]{1,0:T(8,128)S(1)} fusion(bf16[16,2048]{0,1:T(8,128)(2,1)S(1)} %bitcast.110, bf16[2048,2048]{1,0:T(8,128)(2,1)} %reshape.288, f32[16]{0:T(128)S(1)} %convert_bitcast_fusion, f32[2048]{0:T(1024)S(1)} %bitcast.112), kind=kOutput, calls=%fused_computation.3 | convolution fusion | flops 134283264 | bytes 8593472 | tf_op jit(solution)/shard_map/dot_general | solution.py:107
  347.4 0.5 convolution_bitcast_fusion
  347.8 0.4 convolution_bitcast_fusion.1
  348.3 0.5 fusion.20
  348.8 0.5 fusion.19
  349.3 0.5 fusion.8
  350.3 0.5 fusion.7
  351.2 0.6 multiply_subtract_fusion.2
  351.9 1.0 copy.35
  352.9 3.6 reshape.332
  356.5 10.6 %all-to-all-start.2 = ((f32[128,1,512]{2,1,0:T(1,128)}), f32[128,1,512]{2,1,0:T(1,128)S(1)}, u32[]{:S(2)}, u32[]{:S(2)}) async-start(f32[128,1,512]{2,1,0:T(1,128)} %reshape.332), calls=%async_computation.2 | async-start | bytes 524288 | tf_op jit(solution)/shard_map/all_to_all | solution.py:119
  367.1 0.6 broadcast.269
  367.7 0.7 fusion.127
  368.7 13.5 %all-to-all-done.2 = f32[128,1,512]{2,1,0:T(1,128)S(1)} async-done(((f32[128,1,512]{2,1,0:T(1,128)}), f32[128,1,512]{2,1,0:T(1,128)S(1)}, u32[]{:S(2)}, u32[]{:S(2)}) %all-to-all-start.2) | async-done | bytes 262176 | tf_op jit(solution)/shard_map/all_to_all | solution.py:119
  382.2 0.5 broadcast.270
  382.8 1.2 reduce.9
  384.0 2.8 reshape.333
  386.8 2.6 copy.51
  389.4 3.2 copy.46
  392.6 3.6 reshape.334
  396.2 3.6 all-to-all-start.3
  399.9 6.0 %all-to-all-done.3 = f32[4,1,16384]{2,1,0:T(1,128)S(1)} async-done(((f32[4,1,16384]{2,1,0:T(1,128)}), f32[4,1,16384]{2,1,0:T(1,128)S(1)}, u32[]{:S(2)}, u32[]{:S(2)}) %all-to-all-start.3) | async-done | bytes 262176 | tf_op jit(solution)/shard_map/all_to_all | solution.py:118
  405.9 1.3 reduce.10
  407.2 2.8 reshape.335
  410.0 2.5 fusion.128
  412.5 1.6 copy.47
  414.5 0.4 fusion.41
  415.4 0.4 convolution_subtract_fusion.1
  416.3 0.5 fusion.22
  416.8 0.5 fusion.21
  417.3 0.5 fusion.6
  418.2 0.5 fusion.4
  419.1 0.6 gather_fusion
  419.8 9.5 %all_gather.11 = f32[128,256]{1,0:T(8,128)S(1)} all-gather(f32[32,256]{1,0:T(8,128)S(1)} %broadcast_select_fusion), channel_id=1, replica_groups=mesh['row'=128,'ex'=4] {'ex'}, dimensions={0}, use_global_device_ids=true | all-gather | bytes 163840 | tf_op jit(solution)/shard_map/all_gather | solution.py:133
  429.3 1.1 scatter_custom_fusion
  430.5 24.0 %all_to_all.57 = f32[128,2,256]{2,1,0:T(2,128)S(1)} all-to-all(f32[128,2,256]{2,1,0:T(2,128)S(1)} %all_to_all.49), channel_id=1, replica_groups=mesh['row'=128,'ex'=4] {'row'}, dimensions={0} | all-to-all | bytes 524288 | tf_op jit(solution)/shard_map/all_to_all | solution.py:139
  454.4 0.7 copy.54
  (37 shorter events, 5.1 us)
Async XLA Ops:
  6.5 92.9 %all-gather.3.cloned.1.call-start = ((), (), s32[]{:S(2)}) async-start(), calls=%async_computation.5 | async-start | bytes 2113536 | tf_op jit(solution)/shard_map/all_gather | solution.py:81
  101.5 21.9 %copy-start = (bf16[4,2048]{1,0:T(4,128)(2,1)S(1)}, bf16[4,2048]{1,0:T(4,128)(2,1)}, u32[]{:S(2)}) copy-start(bf16[4,2048]{1,0:T(4,128)(2,1)} %param.9) | copy-start | bytes 49156
  131.0 13.2 %copy-start.2 = (s32[1,1,1,32]{3,2,1,0:T(1,128)S(1)}, s32[1,1,1,32]{3,2,1,0:T(1,128)}, u32[]{:S(2)}) copy-start(s32[1,1,1,32]{3,2,1,0:T(1,128)} %param.12) | copy-start | bytes 388
  131.0 198.2 %all-to-all-start.1 = ((bf16[512,4,2048]{2,1,0:T(4,128)(2,1)}), bf16[512,4,2048]{2,1,0:T(4,128)(2,1)}, u32[]{:S(2)}, u32[]{:S(2)}) async-start(bf16[512,4,2048]{2,1,0:T(4,128)(2,1)} %stack.4), calls=%async_computation.1 | async-start | bytes 16777216 | tf_op jit(solution)/shard_map/all_to_all | solution.py:83
  351.8 15.9 %copy-start.1 = (s32[1,1,4,32,1]{3,4,2,1,0:T(1,128)S(1)}, s32[1,1,4,32,1]{3,4,2,1,0:T(1,128)}, u32[]{:S(2)}) copy-start(s32[1,1,4,32,1]{3,4,2,1,0:T(1,128)} %param.13) | copy-start | bytes 1540
  356.5 25.7 %all-to-all-start.2 = ((f32[128,1,512]{2,1,0:T(1,128)}), f32[128,1,512]{2,1,0:T(1,128)S(1)}, u32[]{:S(2)}, u32[]{:S(2)}) async-start(f32[128,1,512]{2,1,0:T(1,128)} %reshape.332), calls=%async_computation.2 | async-start | bytes 524288 | tf_op jit(solution)/shard_map/all_to_all | solution.py:119
  396.2 9.7 %all-to-all-start.3 = ((f32[4,1,16384]{2,1,0:T(1,128)}), f32[4,1,16384]{2,1,0:T(1,128)S(1)}, u32[]{:S(2)}, u32[]{:S(2)}) async-start(f32[4,1,16384]{2,1,0:T(1,128)} %reshape.334), calls=%async_computation.3 | async-start | bytes 524288 | tf_op jit(solution)/shard_map/all_to_all | solution.py:118
Sparse Core Ops, SparseCore 0:
  10.5 88.9 all-gather.2
